TPU v7x, 256 devices: a whole 4x4x8 slice. The times are simulated.
256 devices in a mesh: seq: 32 (over x, z), chan: 8 (over y, core).
Axes of the slice: x: 4, y: 4, z: 8, core: 2. Of those that a mesh axis runs over, the one named last changes fastest.
Arguments:
- query_rows: bfloat16 [8192, 2048], P('seq', 'chan'), may hold values from -6 to 6
- key_rows: bfloat16 [8192, 2048], P('seq', 'chan'), may hold values from -6 to 6
- value_rows: bfloat16 [8192, 2048], P('seq', 'chan'), may hold values from -6 to 6
- long_filter: float32 [8192, 2048], P('seq', 'chan'), may hold values from -2 to 2
- short_taps: float32 [3, 3, 2048], P(None, None, ('seq', 'chan')), may hold values from -3 to 3
- skip_gain: float32 [2048], P(('seq', 'chan')), may hold values from -3 to 3
- cotangent: bfloat16 [8192, 2048], P('seq', 'chan'), may hold values from -6 to 6
Outputs:
- gated_out: bfloat16 [8192, 2048], P('seq', 'chan')
- query_grad: bfloat16 [8192, 2048], P('seq', 'chan')
- key_grad: bfloat16 [8192, 2048], P('seq', 'chan')
- value_grad: bfloat16 [8192, 2048], P('seq', 'chan')
- filter_grad: float32 [8192, 2048], P('seq', 'chan')
- taps_grad: float32 [3, 3, 2048], P(None, None, 'chan')
- skip_grad: float32 [2048], P('chan')
All inputs are finite; a program needn't handle non-finite values.
Results may differ from a plain program's by a relative error of at most 0.00135.
Values may be sent and summed in bfloat16 or wider, within the bound.
A program may use at most 64 MiB of HBM per device.

v0:
```python
import math
import jax
import jax.numpy as jnp
from jax import lax
from jax.sharding import PartitionSpec as P

exact_dot = lax.Precision.HIGHEST


def from_behind(value, axis, by):
    length = lax.axis_size(axis)
    pairs = [(i, i + by) for i in range(length) if 0 <= i + by < length]
    return lax.ppermute(value, axis, pairs)


def angles(left_index, right_index, period):
    product = left_index[:, None] * right_index[None, :] % period
    return 2.0 * math.pi / period * product.astype(jnp.float32)


def source_transform(pieces, row_start, total):
    sources = pieces.shape[1]
    row_count = pieces.shape[2]
    source_index = jnp.arange(sources, dtype=jnp.int32)
    freq_index = jnp.arange(2 * sources, dtype=jnp.int32)
    theta = angles(source_index, freq_index, 2 * sources)
    real_part = jnp.einsum("fqrc,qk->fkrc", pieces, jnp.cos(theta), precision=exact_dot)
    imag_part = -jnp.einsum("fqrc,qk->fkrc", pieces, jnp.sin(theta), precision=exact_dot)
    row_index = row_start + jnp.arange(row_count, dtype=jnp.int32)
    twist = angles(freq_index, row_index, total)
    cosine = jnp.cos(twist)[None, :, :, None]
    sine = jnp.sin(twist)[None, :, :, None]
    return jnp.stack([real_part * cosine + imag_part * sine, imag_part * cosine - real_part * sine])


def row_transform(spectra, direction):
    length = spectra.shape[3]
    positions = jnp.arange(length, dtype=jnp.int32)
    theta = angles(positions, positions, length)
    cosine = jnp.cos(theta)
    sine = jnp.sin(theta)
    real_cos = jnp.einsum("femc,mk->fekc", spectra[0], cosine, precision=exact_dot)
    real_sin = jnp.einsum("femc,mk->fekc", spectra[0], sine, precision=exact_dot)
    imag_cos = jnp.einsum("femc,mk->fekc", spectra[1], cosine, precision=exact_dot)
    imag_sin = jnp.einsum("femc,mk->fekc", spectra[1], sine, precision=exact_dot)
    return jnp.stack([real_cos - direction * imag_sin, imag_cos + direction * real_sin])


def untwist(spectra, freq_start, total):
    freq_index = freq_start + jnp.arange(spectra.shape[2], dtype=jnp.int32)
    row_index = jnp.arange(spectra.shape[3], dtype=jnp.int32)
    twist = angles(freq_index, row_index, total)
    cosine = jnp.cos(twist)[None, :, :, None]
    sine = jnp.sin(twist)[None, :, :, None]
    return jnp.stack(
        [spectra[0] * cosine - spectra[1] * sine, spectra[1] * cosine + spectra[0] * sine]
    )


def source_sum(spectra, total):
    freqs = spectra.shape[2]
    theta = angles(
        jnp.arange(freqs // 2, dtype=jnp.int32), jnp.arange(freqs, dtype=jnp.int32), freqs
    )
    summed = jnp.einsum("fkrc,qk->fqrc", spectra[0], jnp.cos(theta), precision=exact_dot)
    summed = summed - jnp.einsum("fkrc,qk->fqrc", spectra[1], jnp.sin(theta), precision=exact_dot)
    return summed / total


def spectrum_split(fields):
    devices = lax.axis_size("seq")
    place = lax.axis_index("seq")
    nfields, row_count, channels = fields.shape
    share = row_count // devices
    total = 2 * devices * row_count
    mixed = source_transform(
        lax.all_to_all(
            fields.reshape(nfields, 1, row_count, channels),
            "seq",
            split_axis=2,
            concat_axis=1,
            tiled=True,
        ),
        place * share,
        total,
    )
    mixed = mixed.reshape(2, nfields, devices, 2, share, channels)
    return row_transform(
        lax.all_to_all(mixed, "seq", split_axis=2, concat_axis=4, tiled=True)[:, :, 0], -1.0
    )


def signal_split(spectra):
    devices = lax.axis_size("seq")
    place = lax.axis_index("seq")
    nfields = spectra.shape[1]
    row_count = spectra.shape[3]
    channels = spectra.shape[4]
    share = row_count // devices
    total = 2 * devices * row_count
    turned = untwist(row_transform(spectra, 1.0), 2 * place, total)
    turned = turned.reshape(2, nfields, 1, 2, devices, share, channels)
    pieces = lax.all_to_all(turned, "seq", split_axis=4, concat_axis=2, tiled=True)
    gathered = source_sum(pieces.reshape(2, nfields, 2 * devices, share, pieces.shape[6]), total)
    return lax.all_to_all(gathered, "seq", split_axis=1, concat_axis=2, tiled=True).reshape(
        nfields, row_count, channels
    )


def complex_product(left, right, conjugate):
    right_imag = -right[1] if conjugate else right[1]
    return jnp.stack(
        [left[0] * right[0] - left[1] * right_imag, left[0] * right_imag + left[1] * right[0]]
    )


def per_device(query_rows, key_rows, value_rows, long_filter, short_taps, skip_gain, cotangent):
    row_count, channels = query_rows.shape
    devices = lax.axis_size("seq")
    grad_scale = 1.0 / math.sqrt(row_count * devices)
    all_taps, all_gain = (
        lax.all_gather(short_taps, ("seq", "chan"), axis=2, tiled=True),
        lax.all_gather(skip_gain, ("seq", "chan"), axis=0, tiled=True),
    )
    start = lax.axis_index("chan") * channels
    tap_block = lax.dynamic_slice_in_dim(all_taps, start, channels, 2)
    skip_block = lax.dynamic_slice_in_dim(all_gain, start, channels, 0)
    streams = jnp.stack([query_rows, key_rows, value_rows])
    lower = from_behind(streams[:, row_count - 2 :, :], "seq", 1)
    extended = jnp.concatenate([lower, streams], axis=1).astype(jnp.float32)
    shorted = sum(
        (
            tap_block[:, offset, None, :] * extended[:, 2 - offset : 2 - offset + row_count]
            for offset in range(3)
        )
    )
    query_conv = shorted[0]
    key_conv = shorted[1]
    value_conv = shorted[2]
    product = key_conv * value_conv
    upstream = cotangent.astype(jnp.float32)
    gated_grad = upstream * query_conv
    spectra = spectrum_split(jnp.stack([product, long_filter]))
    prod_spec = spectra[:, 0]
    filt_spec = spectra[:, 1]
    conv_part = signal_split(complex_product(prod_spec, filt_spec, False)[:, None])[0]
    grad_spec = spectrum_split(gated_grad[None])[:, 0]
    back = signal_split(
        jnp.stack(
            [
                complex_product(grad_spec, filt_spec, True),
                complex_product(grad_spec, prod_spec, True),
            ],
            axis=1,
        )
    )
    corr_product = back[0]
    corr_filter = back[1]
    mixed_conv = conv_part + skip_block * product
    gated_out = (query_conv * mixed_conv).astype(jnp.bfloat16)
    query_conv_grad = upstream * mixed_conv
    product_grad = corr_product + skip_block * gated_grad
    filter_grad = grad_scale * corr_filter
    key_conv_grad = product_grad * value_conv
    value_conv_grad = product_grad * key_conv
    conv_grads = jnp.stack([query_conv_grad, key_conv_grad, value_conv_grad])
    upper = from_behind(conv_grads[:, :2, :], "seq", -1)
    ext_grads = jnp.concatenate([conv_grads, upper], axis=1)
    input_grads = sum(
        (
            tap_block[:, offset, None, :] * ext_grads[:, offset : offset + row_count]
            for offset in range(3)
        )
    ).astype(jnp.bfloat16)
    tap_terms = jnp.stack(
        [
            jnp.sum(conv_grads * extended[:, 2 - offset : 2 - offset + row_count], axis=1)
            for offset in range(3)
        ],
        axis=1,
    )
    skip_terms = jnp.sum(gated_grad * product, axis=0)
    tap_total, skip_total = lax.psum((tap_terms, skip_terms), "seq")
    return (
        gated_out,
        input_grads[0],
        input_grads[1],
        input_grads[2],
        filter_grad,
        grad_scale * tap_total,
        grad_scale * skip_total,
    )


def solution(mesh):
    in_specs = (
        P("seq", "chan"),
        P("seq", "chan"),
        P("seq", "chan"),
        P("seq", "chan"),
        P(None, None, ("seq", "chan")),
        P(("seq", "chan")),
        P("seq", "chan"),
    )
    out_specs = (
        P("seq", "chan"),
        P("seq", "chan"),
        P("seq", "chan"),
        P("seq", "chan"),
        P("seq", "chan"),
        P(None, None, "chan"),
        P("chan"),
    )
    return jax.shard_map(
        per_device, mesh=mesh, in_specs=in_specs, out_specs=out_specs, check_vma=False
    )
```

profile of v0, /device:TPU:8, one launch (start us, length us, event | category | flops | bytes accessed | tf_op | source)
XLA Modules:
  0.0 597.0 jit_solution(4957405621104877456)
XLA Ops:
  1.4 3.8 collective-permute-start
  6.0 83.8 %all_gather.6 = f32[3,3,2048]{1,0,2:T(4,128)} all-gather(f32[3,3,8]{1,0,2:T(4,128)S(1)} %copy.38), channel_id=1, replica_groups=mesh['seq'=32,'chan'=8] {'seq','chan'}, dimensions={2}, use_global_device_ids=true | all-gather | bytes 74016 | tf_op jit(solution)/shard_map/all_gather | solution.py:122
  89.7 2.1 constant_dynamic-slice_fusion.1
  94.4 7.2 %all-to-all-start.4 = ((f32[1,1,256,256]{3,1,0,2:T(1,128)}), f32[1,1,256,256]{3,1,0,2:T(1,128)S(1)}, u32[]{:S(2)}, u32[]{:S(2)}) async-start(f32[1,1,256,256]{3,1,0,2:T(1,128)} %copy.55), calls=%async_computation.4 | async-start | bytes 524288 | tf_op jit(solution)/shard_map/all_to_all | solution.py:77
  102.9 11.3 %all-to-all-done.4 = f32[1,1,256,256]{3,1,0,2:T(1,128)S(1)} async-done(((f32[1,1,256,256]{3,1,0,2:T(1,128)}), f32[1,1,256,256]{3,1,0,2:T(1,128)S(1)}, u32[]{:S(2)}, u32[]{:S(2)}) %all-to-all-start.4) | async-done | bytes 262176 | tf_op jit(solution)/shard_map/all_to_all | solution.py:77
  114.3 4.7 all-to-all-start
  121.8 1.6 copy.78
  123.4 12.5 %all-to-all-done = f32[2,1,256,256]{3,0,1,2:T(2,128)S(1)} async-done(((f32[2,1,256,256]{3,0,1,2:T(2,128)}), f32[2,1,256,256]{3,0,1,2:T(2,128)S(1)}, u32[]{:S(2)}, u32[]{:S(2)}) %all-to-all-start) | async-done | bytes 524320 | tf_op jit(solution)/shard_map/all_to_all | solution.py:77
  135.9 5.8 all-to-all-start.5
  144.2 1.6 stack.117
  145.8 1.6 stack.118
  147.4 2.7 pad_maximum_fusion
  150.1 2.5 copy.74
  152.7 17.1 %all-to-all-done.5 = f32[2,1,32,2,8,256]{5,3,4,1,0,2:T(2,128)} async-done(((f32[2,1,32,2,8,256]{5,3,4,1,0,2:T(2,128)}), f32[2,1,32,2,8,256]{5,3,4,1,0,2:T(2,128)}, u32[]{:S(2)}, u32[]{:S(2)}) %all-to-all-start.5) | async-done | bytes 1048608 | tf_op jit(solution)/shard_map/all_to_all | solution.py:89
  169.8 4.9 all-to-all-start.1
  174.8 2.4 fusion.254
  177.2 47.1 %all-to-all-done.1 = f32[2,2,32,2,8,256]{5,3,4,1,0,2:T(2,128)S(1)} async-done(((f32[2,2,32,2,8,256]{5,3,4,1,0,2:T(2,128)}), f32[2,2,32,2,8,256]{5,3,4,1,0,2:T(2,128)S(1)}, u32[]{:S(2)}, u32[]{:S(2)}) %all-to-all-start.1) | async-done | bytes 2097184 | tf_op jit(solution)/shard_map/all_to_all | solution.py:89
  225.2 2.0 fusion.23
  227.2 2.0 fusion.19
  229.2 2.1 fusion.5
  231.3 2.1 fusion.3
  233.6 1.6 fusion.45
  235.2 13.2 %fusion.49 = f32[256,2,256]{2,0,1:T(8,128)S(1)} fusion(f32[1,1,2,256,256]{4,3,2,1,0:T(8,128)S(1)} %get-tuple-element.40), kind=kOutput, calls=%fused_computation.91 | convolution fusion | flops 403570688 | bytes 1048576 | tf_op jit(solution)/shard_map/femc,mk->fekc/dot_general | solution.py:42
  248.4 1.6 fusion.12
  250.1 1.8 subtract_bitcast_fusion.2
  253.1 6.2 %all-to-all-start.2 = ((f32[2,1,1,2,32,8,256]{6,5,3,2,1,0,4:T(8,128)}), f32[2,1,1,2,32,8,256]{6,5,3,2,1,0,4:T(8,128)}, u32[]{:S(2)}, u32[]{:S(2)}) async-start(f32[2,1,1,2,32,8,256]{6,5,3,2,1,0,4:T(8,128)} %copy.75), calls=%async_computation.2 | async-start | bytes 2097152 | tf_op jit(solution)/shard_map/all_to_all | solution.py:103
  259.2 1.6 fusion.40
  260.9 2.7 fusion.11
  263.6 1.6 fusion.36
  265.2 2.0 fusion.32
  267.3 2.0 fusion.58
  269.4 2.0 fusion.79
  271.4 2.3 fusion
  273.7 2.3 subtract_bitcast_fusion
  276.2 1.6 copy.79
  277.8 9.7 %all-to-all-done.2 = f32[2,1,1,2,32,8,256]{6,5,3,2,1,0,4:T(8,128)} async-done(((f32[2,1,1,2,32,8,256]{6,5,3,2,1,0,4:T(8,128)}), f32[2,1,1,2,32,8,256]{6,5,3,2,1,0,4:T(8,128)}, u32[]{:S(2)}, u32[]{:S(2)}) %all-to-all-start.2) | async-done | bytes 1048608 | tf_op jit(solution)/shard_map/all_to_all | solution.py:103
  287.5 4.9 all-to-all-start.6
  295.7 46.4 %all-to-all-done.6 = f32[2,2,1,2,32,8,256]{6,5,3,1,2,0,4:T(8,128)S(1)} async-done(((f32[2,2,1,2,32,8,256]{6,5,3,1,2,0,4:T(8,128)}), f32[2,2,1,2,32,8,256]{6,5,3,1,2,0,4:T(8,128)S(1)}, u32[]{:S(2)}, u32[]{:S(2)}) %all-to-all-start.6) | async-done | bytes 2097184 | tf_op jit(solution)/shard_map/all_to_all | solution.py:103
  342.1 6.0 %all-to-all-start.3 = ((f32[1,32,8,256]{3,2,0,1:T(8,128)}), f32[1,32,8,256]{3,2,0,1:T(8,128)S(1)}, u32[]{:S(2)}, u32[]{:S(2)}) async-start(f32[1,32,8,256]{3,2,0,1:T(8,128)} %copy.54), calls=%async_computation.3 | async-start | bytes 524288 | tf_op jit(solution)/shard_map/all_to_all | solution.py:105
  349.3 1.5 copy.65
  350.8 1.9 squeeze.40
  352.7 2.7 copy.64
  355.4 2.9 squeeze.39
  358.4 1.9 fusion.118
  362.2 9.8 %all-to-all-start.7 = ((f32[2,32,8,256]{3,2,0,1:T(8,128)}), f32[2,32,8,256]{3,2,0,1:T(8,128)S(1)}, u32[]{:S(2)}, u32[]{:S(2)}) async-start(f32[2,32,8,256]{3,2,0,1:T(8,128)} %copy.66), calls=%async_computation.7 | async-start | bytes 1048576 | tf_op jit(solution)/shard_map/all_to_all | solution.py:105
  372.3 75.6 %all-reduce = f32[2048]{0:T(1024)S(1)} all-reduce(f32[2048]{0:T(1024)S(1)} %dynamic-update-slice), channel_id=1, replica_groups=mesh['seq'=32,'chan'=8] {'seq','chan'}, use_global_device_ids=true, to_apply=%add | all-reduce | flops 2048 | bytes 16384
  450.8 3.5 collective-permute-done.1
  454.9 139.8 %all-reduce.1 = (f32[3,3,256]{2,0,1:T(4,128)S(1)}, f32[256]{0:T(256)S(1)}) all-reduce(f32[3,3,256]{2,0,1:T(4,128)S(1)} %pad_maximum_fusion.7, f32[256]{0:T(256)S(1)} %get-tuple-element.57), channel_id=1, replica_groups=mesh['seq'=32,'chan'=8] {'seq'}, use_global_device_ids=true, to_apply=%region_3.4 | all-reduce | flops 2560 | bytes 20480 | tf_op jit(solution)/shard_map/psum | solution.py:183
  (78 shorter events, 25.2 us)
Async XLA Ops:
  1.4 91.1 %collective-permute-start = (bf16[3,2,256]{2,1,0:T(2,128)(2,1)S(1)}, bf16[3,2,256]{2,1,0:T(2,128)(2,1)S(1)}, u32[]{:S(2)}, u32[]{:S(2)}) collective-permute-start(bf16[3,2,256]{2,1,0:T(2,128)(2,1)S(1)} %pad_maximum_fusion.8), channel_id=1, source_target_pairs={{0,8},{8,16},{16,24},{24,32},{32,40},{40,48},{48,56},{56,64},{64,7... | collective-permute-start | bytes 9224 | tf_op jit(solution)/shard_map/ppermute | solution.py:13
  89.7 2.7 copy-start.4
  89.7 2.7 copy-start.5
  89.7 2.8 copy-start.6
  92.5 0.9 copy-start.7
  92.6 9.1 %copy-start.9 = (f32[256,256]{1,0:T(8,128)S(1)}, f32[256,256]{1,0:T(8,128)}, u32[]{:S(2)}) copy-start(f32[256,256]{1,0:T(8,128)} %param.10) | copy-start | bytes 786436
  93.4 9.5 %copy-start = (f32[3,256,256]{2,1,0:T(8,128)}, f32[3,256,256]{2,1,0:T(8,128)S(1)}, u32[]{:S(2)}) copy-start(f32[3,256,256]{2,1,0:T(8,128)S(1)} %multiply_add_fusion) | copy-start | bytes 2359300
  94.4 19.9 %all-to-all-start.4 = ((f32[1,1,256,256]{3,1,0,2:T(1,128)}), f32[1,1,256,256]{3,1,0,2:T(1,128)S(1)}, u32[]{:S(2)}, u32[]{:S(2)}) async-start(f32[1,1,256,256]{3,1,0,2:T(1,128)} %copy.55), calls=%async_computation.4 | async-start | bytes 524288 | tf_op jit(solution)/shard_map/all_to_all | solution.py:77
  114.3 21.6 %all-to-all-start = ((f32[2,1,256,256]{3,0,1,2:T(2,128)}), f32[2,1,256,256]{3,0,1,2:T(2,128)S(1)}, u32[]{:S(2)}, u32[]{:S(2)}) async-start(f32[2,1,256,256]{3,0,1,2:T(2,128)} %copy.42), calls=%async_computation | async-start | bytes 1048576 | tf_op jit(solution)/shard_map/all_to_all | solution.py:77
  135.9 33.9 %all-to-all-start.5 = ((f32[2,1,32,2,8,256]{5,3,4,1,0,2:T(2,128)}), f32[2,1,32,2,8,256]{5,3,4,1,0,2:T(2,128)}, u32[]{:S(2)}, u32[]{:S(2)}) async-start(f32[2,1,32,2,8,256]{5,3,4,1,0,2:T(2,128)} %copy.78), calls=%async_computation.5 | async-start | bytes 2097152 | tf_op jit(solution)/shard_map/all_to_all | solution.py:89
  145.8 1.6 copy-start.2
  169.8 54.5 %all-to-all-start.1 = ((f32[2,2,32,2,8,256]{5,3,4,1,0,2:T(2,128)}), f32[2,2,32,2,8,256]{5,3,4,1,0,2:T(2,128)S(1)}, u32[]{:S(2)}, u32[]{:S(2)}) async-start(f32[2,2,32,2,8,256]{5,3,4,1,0,2:T(2,128)} %copy.74), calls=%async_computation.1 | async-start | bytes 4194304 | tf_op jit(solution)/shard_map/all_to_all | solution.py:89
  253.1 34.5 %all-to-all-start.2 = ((f32[2,1,1,2,32,8,256]{6,5,3,2,1,0,4:T(8,128)}), f32[2,1,1,2,32,8,256]{6,5,3,2,1,0,4:T(8,128)}, u32[]{:S(2)}, u32[]{:S(2)}) async-start(f32[2,1,1,2,32,8,256]{6,5,3,2,1,0,4:T(8,128)} %copy.75), calls=%async_computation.2 | async-start | bytes 2097152 | tf_op jit(solution)/shard_map/all_to_all | solution.py:103
  259.2 4.3 copy-start.3
  287.5 54.6 %all-to-all-start.6 = ((f32[2,2,1,2,32,8,256]{6,5,3,1,2,0,4:T(8,128)}), f32[2,2,1,2,32,8,256]{6,5,3,1,2,0,4:T(8,128)S(1)}, u32[]{:S(2)}, u32[]{:S(2)}) async-start(f32[2,2,1,2,32,8,256]{6,5,3,1,2,0,4:T(8,128)} %copy.79), calls=%async_computation.6 | async-start | bytes 4194304 | tf_op jit(solution)/shard_map/all_to_all | solution.py:103
  342.1 20.1 %all-to-all-start.3 = ((f32[1,32,8,256]{3,2,0,1:T(8,128)}), f32[1,32,8,256]{3,2,0,1:T(8,128)S(1)}, u32[]{:S(2)}, u32[]{:S(2)}) async-start(f32[1,32,8,256]{3,2,0,1:T(8,128)} %copy.54), calls=%async_computation.3 | async-start | bytes 524288 | tf_op jit(solution)/shard_map/all_to_all | solution.py:105
  360.3 11.7 %copy-start.10 = (f32[8]{0:T(128)S(1)}, f32[8]{0:T(128)}, u32[]{:S(2)}) copy-start(f32[8]{0:T(128)} %param.12) | copy-start | bytes 100
  360.3 87.6 %copy-start.1 = (f32[3,256,256]{2,1,0:T(8,128)S(1)}, f32[3,256,256]{2,1,0:T(8,128)}, u32[]{:S(2)}) copy-start(f32[3,256,256]{2,1,0:T(8,128)} %copy-done) | copy-start | bytes 2359300
  360.3 87.6 %copy-start.8 = (bf16[256,256]{1,0:T(8,128)(2,1)S(1)}, bf16[256,256]{1,0:T(8,128)(2,1)}, u32[]{:S(2)}) copy-start(bf16[256,256]{1,0:T(8,128)(2,1)} %param.13) | copy-start | bytes 393220
  362.2 85.8 %all-to-all-start.7 = ((f32[2,32,8,256]{3,2,0,1:T(8,128)}), f32[2,32,8,256]{3,2,0,1:T(8,128)S(1)}, u32[]{:S(2)}, u32[]{:S(2)}) async-start(f32[2,32,8,256]{3,2,0,1:T(8,128)} %copy.66), calls=%async_computation.7 | async-start | bytes 1048576 | tf_op jit(solution)/shard_map/all_to_all | solution.py:105
  448.8 5.5 collective-permute-start.1
where the time goes:
time: 606 us; the launch traced here: 597 us
  blocking collectives  299 us (49%)
  waiting for transfers between devices  148 us (24%)
  starting transfers between devices  54.5 us (9%)
  matrix products  50.8 us (8%)
  local copies, waits for them, and re-layouts  35.4 us (6%)
  other arithmetic  7.9 us (1%)
    psum x1, blocking collectives, per_device(): tap_total, skip_total = lax.psum((tap_terms, skip_terms), 'seq')  140 us
    all_gather x1, blocking collectives, per_device(): lax.all_gather(short_taps, ('seq', 'chan'), axis=2, tiled=True)  83.8 us
    unnamed x1, blocking collectives  75.6 us
    all_to_all x2, waiting for transfers between devices, spectrum_split(): lax.all_to_all(mixed, 'seq', split_axis=2, concat_axis=4, tiled=True)  64.2 us
    all_to_all x2, waiting for transfers between devices, signal_split(): lax.all_to_all(turned, 'seq', split_axis=4, concat_axis=2, tiled=True)  56.1 us
    all_to_all x2, waiting for transfers between devices, spectrum_split(): lax.all_to_all(fields.reshape(nfields, 1, row_count, channels), 'seq', sp...  23.8 us
    dot_general x4, matrix products, row_transform(): jnp.einsum('femc,mk->fekc', spectra[0], cosine, precision=exact_dot)  18.9 us
    all_to_all x2, starting transfers between devices, signal_split(): lax.all_to_all(gathered, 'seq', split_axis=1, concat_axis=2, tiled=True)  15.8 us
  transfers between devices with their start and end apart: 10, of which 7 were waited for; matrix products, arithmetic and copies ran while one was open for 10% of the time, Pallas kernels for 0%

commit v1 on v0

--- a/solution.py
+++ b/solution.py
@@ -119,7 +119,12 @@
     devices = lax.axis_size("seq")
     grad_scale = 1.0 / math.sqrt(row_count * devices)
     all_taps, all_gain = (
-        lax.all_gather(short_taps, ("seq", "chan"), axis=2, tiled=True),
+        jnp.concatenate(
+            lax.all_to_all(
+                jnp.stack([short_taps] * lax.axis_size(("seq", "chan"))), ("seq", "chan"), 0, 0
+            ),
+            axis=2,
+        ),
         lax.all_gather(skip_gain, ("seq", "chan"), axis=0, tiled=True),
     )
     start = lax.axis_index("chan") * channels

time: 606 us -> 562 us (0.927)
  blocking collectives: 299 us -> 214 us
  waiting for transfers between devices: 148 us -> 176 us
  starting transfers between devices: 54.5 us -> 64.6 us
    all_gather x1 -> x0, blocking collectives: 83.8 us -> none  [per_device(): lax.all_gather(short_taps, ('seq', 'chan'), axis=2, tiled=True)]
    ppermute x2, waiting for transfers between devices: 3.5 us -> 29.1 us  [from_behind(): return lax.ppermute(value, axis, pairs)]
    all_to_all x0 -> x1, starting transfers between devices: none -> 14.6 us  [per_device(): lax.all_to_all(jnp.stack([short_taps] * lax.axis_size(('seq', 'chan'))),...]
    dot_general x4, matrix products: 7.3 us -> 21 us  [row_transform(): jnp.einsum('femc,mk->fekc', spectra[1], cosine, precision=exact_dot)]
    all_to_all x0 -> x1, waiting for transfers between devices: none -> 13.2 us  [per_device(): lax.all_to_all(jnp.stack([short_taps] * lax.axis_size(('seq', 'chan'))),...]
    dot_general x4, matrix products: 18.9 us -> 8.14 us  [row_transform(): jnp.einsum('femc,mk->fekc', spectra[0], cosine, precision=exact_dot)]
  transfers between devices with their start and end apart: 10 -> 11, of which waited for: 7 -> 9; matrix products, arithmetic and copies ran while one was open for 10% -> 11% of each run, Pallas kernels for 0% -> 0%
where the time goes in v1:
time: 562 us; the launch traced here: 555 us
  blocking collectives  214 us (38%)
  waiting for transfers between devices  176 us (31%)
  starting transfers between devices  64.6 us (11%)
  matrix products  53.8 us (10%)
  local copies, waits for them, and re-layouts  36.8 us (7%)
  other arithmetic  7.29 us (1%)
    psum x1, blocking collectives, per_device(): tap_total, skip_total = lax.psum((tap_terms, skip_terms), 'seq')  139 us
    unnamed x1, blocking collectives  74.7 us
    all_to_all x2, waiting for transfers between devices, spectrum_split(): lax.all_to_all(mixed, 'seq', split_axis=2, concat_axis=4, tiled=True)  58.9 us
    all_to_all x2, waiting for transfers between devices, signal_split(): lax.all_to_all(turned, 'seq', split_axis=4, concat_axis=2, tiled=True)  52.3 us
    ppermute x2, waiting for transfers between devices, from_behind(): return lax.ppermute(value, axis, pairs)  29.1 us
    all_to_all x2, waiting for transfers between devices, spectrum_split(): lax.all_to_all(fields.reshape(nfields, 1, row_count, channels), 'seq', sp...  22.7 us
    dot_general x4, matrix products, row_transform(): jnp.einsum('femc,mk->fekc', spectra[1], cosine, precision=exact_dot)  21 us
    all_to_all x2, starting transfers between devices, signal_split(): lax.all_to_all(gathered, 'seq', split_axis=1, concat_axis=2, tiled=True)  15.2 us
  transfers between devices with their start and end apart: 11, of which 9 were waited for; matrix products, arithmetic and copies ran while one was open for 11% of the time, Pallas kernels for 0%

profile of v1, /device:TPU:8, one launch (start us, length us, event | category | flops | bytes accessed | tf_op | source)
XLA Modules:
  0.0 554.5 jit_solution(1014714905160768524)
XLA Ops:
  0.7 2.1 stack.68
  2.8 14.6 %all-to-all-start = ((f32[256,3,3,8]{3,2,1,0:T(4,128)}), f32[256,3,3,8]{3,2,1,0:T(4,128)S(1)}, u32[]{:S(2)}, u32[]{:S(2)}) async-start(f32[256,3,3,8]{3,2,1,0:T(4,128)} %stack.68), calls=%async_computation | async-start | bytes 3145728 | tf_op jit(solution)/shard_map/all_to_all | solution.py:123
  17.5 3.6 collective-permute-start
  21.0 25.6 %collective-permute-done = bf16[3,2,256]{2,1,0:T(2,128)(2,1)S(1)} collective-permute-done((bf16[3,2,256]{2,1,0:T(2,128)(2,1)S(1)}, bf16[3,2,256]{2,1,0:T(2,128)(2,1)S(1)}, u32[]{:S(2)}, u32[]{:S(2)}) %collective-permute-start) | collective-permute-done | bytes 3104 | tf_op jit(solution)/shard_map/ppermute | solution.py:13
  46.7 13.2 %all-to-all-done = f32[256,3,3,8]{3,2,1,0:T(4,128)S(1)} async-done(((f32[256,3,3,8]{3,2,1,0:T(4,128)}), f32[256,3,3,8]{3,2,1,0:T(4,128)S(1)}, u32[]{:S(2)}, u32[]{:S(2)}) %all-to-all-start) | async-done | bytes 73760 | tf_op jit(solution)/shard_map/all_to_all | solution.py:123
  61.0 1.9 reshape.301
  64.4 3.9 all-to-all-start.5
  69.7 11.0 %all-to-all-done.5 = f32[1,1,256,256]{3,1,0,2:T(1,128)S(1)} async-done(((f32[1,1,256,256]{3,1,0,2:T(1,128)}), f32[1,1,256,256]{3,1,0,2:T(1,128)S(1)}, u32[]{:S(2)}, u32[]{:S(2)}) %all-to-all-start.5) | async-done | bytes 262176 | tf_op jit(solution)/shard_map/all_to_all | solution.py:77
  80.7 4.4 all-to-all-start.1
  89.5 11.7 %all-to-all-done.1 = f32[2,1,256,256]{3,0,1,2:T(2,128)S(1)} async-done(((f32[2,1,256,256]{3,0,1,2:T(2,128)}), f32[2,1,256,256]{3,0,1,2:T(2,128)S(1)}, u32[]{:S(2)}, u32[]{:S(2)}) %all-to-all-start.1) | async-done | bytes 524320 | tf_op jit(solution)/shard_map/all_to_all | solution.py:77
  101.2 5.6 %all-to-all-start.6 = ((f32[2,1,32,2,8,256]{5,3,4,1,0,2:T(2,128)}), f32[2,1,32,2,8,256]{5,3,4,1,0,2:T(2,128)}, u32[]{:S(2)}, u32[]{:S(2)}) async-start(f32[2,1,32,2,8,256]{5,3,4,1,0,2:T(2,128)} %copy.76), calls=%async_computation.6 | async-start | bytes 2097152 | tf_op jit(solution)/shard_map/all_to_all | solution.py:89
  111.0 1.6 stack.76
  112.6 2.7 pad_maximum_fusion
  115.4 2.6 copy.72
  117.9 16.0 %all-to-all-done.6 = f32[2,1,32,2,8,256]{5,3,4,1,0,2:T(2,128)} async-done(((f32[2,1,32,2,8,256]{5,3,4,1,0,2:T(2,128)}), f32[2,1,32,2,8,256]{5,3,4,1,0,2:T(2,128)}, u32[]{:S(2)}, u32[]{:S(2)}) %all-to-all-start.6) | async-done | bytes 1048608 | tf_op jit(solution)/shard_map/all_to_all | solution.py:89
  133.9 5.4 all-to-all-start.2
  139.4 2.4 fusion.254
  141.8 2.5 fusion.40
  144.2 43.0 %all-to-all-done.2 = f32[2,2,32,2,8,256]{5,3,4,1,0,2:T(2,128)S(1)} async-done(((f32[2,2,32,2,8,256]{5,3,4,1,0,2:T(2,128)}), f32[2,2,32,2,8,256]{5,3,4,1,0,2:T(2,128)S(1)}, u32[]{:S(2)}, u32[]{:S(2)}) %all-to-all-start.2) | async-done | bytes 2097184 | tf_op jit(solution)/shard_map/all_to_all | solution.py:89
  188.0 2.0 fusion.23
  190.1 2.0 fusion.19
  192.1 2.1 fusion.5
  194.2 2.1 fusion.3
  196.4 14.3 %fusion.45 = f32[256,2,256]{2,0,1:T(8,128)S(1)} fusion(f32[1,1,2,256,256]{4,3,2,1,0:T(8,128)S(1)} %get-tuple-element.36), kind=kOutput, calls=%fused_computation.87 | convolution fusion | flops 403570688 | bytes 1048576 | tf_op jit(solution)/shard_map/femc,mk->fekc/dot_general | solution.py:44
  210.7 1.6 fusion.49
  212.3 1.6 fusion.12
  213.9 1.8 subtract_bitcast_fusion.2
  217.0 5.6 %all-to-all-start.3 = ((f32[2,1,1,2,32,8,256]{6,5,3,2,1,0,4:T(8,128)}), f32[2,1,1,2,32,8,256]{6,5,3,2,1,0,4:T(8,128)}, u32[]{:S(2)}, u32[]{:S(2)}) async-start(f32[2,1,1,2,32,8,256]{6,5,3,2,1,0,4:T(8,128)} %copy.73), calls=%async_computation.3 | async-start | bytes 2097152 | tf_op jit(solution)/shard_map/all_to_all | solution.py:103
  222.6 2.8 fusion.11
  225.4 2.7 fusion.36
  228.1 2.0 fusion.32
  230.2 2.0 fusion.58
  232.3 2.0 fusion.79
  234.3 2.1 fusion
  236.4 2.5 subtract_bitcast_fusion
  239.1 1.6 copy.77
  240.8 8.0 %all-to-all-done.3 = f32[2,1,1,2,32,8,256]{6,5,3,2,1,0,4:T(8,128)} async-done(((f32[2,1,1,2,32,8,256]{6,5,3,2,1,0,4:T(8,128)}), f32[2,1,1,2,32,8,256]{6,5,3,2,1,0,4:T(8,128)}, u32[]{:S(2)}, u32[]{:S(2)}) %all-to-all-start.3) | async-done | bytes 1048608 | tf_op jit(solution)/shard_map/all_to_all | solution.py:103
  248.8 5.1 all-to-all-start.7
  257.1 44.3 %all-to-all-done.7 = f32[2,2,1,2,32,8,256]{6,5,3,1,2,0,4:T(8,128)S(1)} async-done(((f32[2,2,1,2,32,8,256]{6,5,3,1,2,0,4:T(8,128)}), f32[2,2,1,2,32,8,256]{6,5,3,1,2,0,4:T(8,128)S(1)}, u32[]{:S(2)}, u32[]{:S(2)}) %all-to-all-start.7) | async-done | bytes 2097184 | tf_op jit(solution)/shard_map/all_to_all | solution.py:103
  301.5 5.4 all-to-all-start.4
  309.6 1.9 squeeze.40
  311.5 2.7 copy.62
  314.2 2.9 squeeze.39
  317.2 1.9 fusion.118
  321.0 9.8 %all-to-all-start.8 = ((f32[2,32,8,256]{3,2,0,1:T(8,128)}), f32[2,32,8,256]{3,2,0,1:T(8,128)S(1)}, u32[]{:S(2)}, u32[]{:S(2)}) async-start(f32[2,32,8,256]{3,2,0,1:T(8,128)} %copy.64), calls=%async_computation.8 | async-start | bytes 1048576 | tf_op jit(solution)/shard_map/all_to_all | solution.py:105
  331.1 74.7 %all-reduce = f32[2048]{0:T(1024)S(1)} all-reduce(f32[2048]{0:T(1024)S(1)} %dynamic-update-slice), channel_id=1, replica_groups=mesh['seq'=32,'chan'=8] {'seq','chan'}, use_global_device_ids=true, to_apply=%add | all-reduce | flops 2048 | bytes 16384
  408.8 3.5 collective-permute-done.1
  412.9 139.3 %all-reduce.1 = (f32[3,3,256]{2,0,1:T(4,128)S(1)}, f32[256]{0:T(256)S(1)}) all-reduce(f32[3,3,256]{2,0,1:T(4,128)S(1)} %pad_maximum_fusion.7, f32[256]{0:T(256)S(1)} %get-tuple-element.54), channel_id=1, replica_groups=mesh['seq'=32,'chan'=8] {'seq'}, use_global_device_ids=true, to_apply=%region_3.4 | all-reduce | flops 2560 | bytes 20480 | tf_op jit(solution)/shard_map/psum | solution.py:188
  (79 shorter events, 28.6 us)
Async XLA Ops:
  0.6 16.8 %copy-start.3 = (bf16[256,256]{1,0:T(8,128)(2,1)S(1)}, bf16[256,256]{1,0:T(8,128)(2,1)}, u32[]{:S(2)}) copy-start(bf16[256,256]{1,0:T(8,128)(2,1)} %param.9) | copy-start | bytes 393220
  0.6 16.8 %copy-start.4 = (bf16[256,256]{1,0:T(8,128)(2,1)S(1)}, bf16[256,256]{1,0:T(8,128)(2,1)}, u32[]{:S(2)}) copy-start(bf16[256,256]{1,0:T(8,128)(2,1)} %param.8) | copy-start | bytes 393220
  0.7 16.8 %copy-start.5 = (bf16[256,256]{1,0:T(8,128)(2,1)S(1)}, bf16[256,256]{1,0:T(8,128)(2,1)}, u32[]{:S(2)}) copy-start(bf16[256,256]{1,0:T(8,128)(2,1)} %param.7) | copy-start | bytes 393220
  2.8 57.1 %all-to-all-start = ((f32[256,3,3,8]{3,2,1,0:T(4,128)}), f32[256,3,3,8]{3,2,1,0:T(4,128)S(1)}, u32[]{:S(2)}, u32[]{:S(2)}) async-start(f32[256,3,3,8]{3,2,1,0:T(4,128)} %stack.68), calls=%async_computation | async-start | bytes 3145728 | tf_op jit(solution)/shard_map/all_to_all | solution.py:123
  17.5 29.2 %collective-permute-start = (bf16[3,2,256]{2,1,0:T(2,128)(2,1)S(1)}, bf16[3,2,256]{2,1,0:T(2,128)(2,1)S(1)}, u32[]{:S(2)}, u32[]{:S(2)}) collective-permute-start(bf16[3,2,256]{2,1,0:T(2,128)(2,1)S(1)} %pad_maximum_fusion.8), channel_id=1, source_target_pairs={{0,8},{8,16},{16,24},{24,32},{32,40},{40,48},{48,56},{56,64},{64,7... | collective-permute-start | bytes 9224 | tf_op jit(solution)/shard_map/ppermute | solution.py:13
  61.0 2.3 copy-start.6
  63.1 5.3 copy-start.8
  63.4 6.3 %copy-start = (f32[3,256,256]{2,1,0:T(8,128)}, f32[3,256,256]{2,1,0:T(8,128)S(1)}, u32[]{:S(2)}) copy-start(f32[3,256,256]{2,1,0:T(8,128)S(1)} %multiply_add_fusion) | copy-start | bytes 2359300
  64.4 16.3 %all-to-all-start.5 = ((f32[1,1,256,256]{3,1,0,2:T(1,128)}), f32[1,1,256,256]{3,1,0,2:T(1,128)S(1)}, u32[]{:S(2)}, u32[]{:S(2)}) async-start(f32[1,1,256,256]{3,1,0,2:T(1,128)} %copy.53), calls=%async_computation.5 | async-start | bytes 524288 | tf_op jit(solution)/shard_map/all_to_all | solution.py:77
  80.7 20.6 %all-to-all-start.1 = ((f32[2,1,256,256]{3,0,1,2:T(2,128)}), f32[2,1,256,256]{3,0,1,2:T(2,128)S(1)}, u32[]{:S(2)}, u32[]{:S(2)}) async-start(f32[2,1,256,256]{3,0,1,2:T(2,128)} %copy.40), calls=%async_computation.1 | async-start | bytes 1048576 | tf_op jit(solution)/shard_map/all_to_all | solution.py:77
  101.2 32.7 %all-to-all-start.6 = ((f32[2,1,32,2,8,256]{5,3,4,1,0,2:T(2,128)}), f32[2,1,32,2,8,256]{5,3,4,1,0,2:T(2,128)}, u32[]{:S(2)}, u32[]{:S(2)}) async-start(f32[2,1,32,2,8,256]{5,3,4,1,0,2:T(2,128)} %copy.76), calls=%async_computation.6 | async-start | bytes 2097152 | tf_op jit(solution)/shard_map/all_to_all | solution.py:89
  111.0 1.6 copy-start.2
  133.9 53.3 %all-to-all-start.2 = ((f32[2,2,32,2,8,256]{5,3,4,1,0,2:T(2,128)}), f32[2,2,32,2,8,256]{5,3,4,1,0,2:T(2,128)S(1)}, u32[]{:S(2)}, u32[]{:S(2)}) async-start(f32[2,2,32,2,8,256]{5,3,4,1,0,2:T(2,128)} %copy.72), calls=%async_computation.2 | async-start | bytes 4194304 | tf_op jit(solution)/shard_map/all_to_all | solution.py:89
  217.0 31.8 %all-to-all-start.3 = ((f32[2,1,1,2,32,8,256]{6,5,3,2,1,0,4:T(8,128)}), f32[2,1,1,2,32,8,256]{6,5,3,2,1,0,4:T(8,128)}, u32[]{:S(2)}, u32[]{:S(2)}) async-start(f32[2,1,1,2,32,8,256]{6,5,3,2,1,0,4:T(8,128)} %copy.73), calls=%async_computation.3 | async-start | bytes 2097152 | tf_op jit(solution)/shard_map/all_to_all | solution.py:103
  248.8 52.7 %all-to-all-start.7 = ((f32[2,2,1,2,32,8,256]{6,5,3,1,2,0,4:T(8,128)}), f32[2,2,1,2,32,8,256]{6,5,3,1,2,0,4:T(8,128)S(1)}, u32[]{:S(2)}, u32[]{:S(2)}) async-start(f32[2,2,1,2,32,8,256]{6,5,3,1,2,0,4:T(8,128)} %copy.77), calls=%async_computation.7 | async-start | bytes 4194304 | tf_op jit(solution)/shard_map/all_to_all | solution.py:103
  301.5 19.5 %all-to-all-start.4 = ((f32[1,32,8,256]{3,2,0,1:T(8,128)}), f32[1,32,8,256]{3,2,0,1:T(8,128)S(1)}, u32[]{:S(2)}, u32[]{:S(2)}) async-start(f32[1,32,8,256]{3,2,0,1:T(8,128)} %copy.52), calls=%async_computation.4 | async-start | bytes 524288 | tf_op jit(solution)/shard_map/all_to_all | solution.py:105
  319.1 11.7 %copy-start.9 = (f32[8]{0:T(128)S(1)}, f32[8]{0:T(128)}, u32[]{:S(2)}) copy-start(f32[8]{0:T(128)} %param.12) | copy-start | bytes 100
  319.1 86.8 %copy-start.1 = (f32[3,256,256]{2,1,0:T(8,128)S(1)}, f32[3,256,256]{2,1,0:T(8,128)}, u32[]{:S(2)}) copy-start(f32[3,256,256]{2,1,0:T(8,128)} %copy-done) | copy-start | bytes 2359300
  319.1 86.8 %copy-start.7 = (bf16[256,256]{1,0:T(8,128)(2,1)S(1)}, bf16[256,256]{1,0:T(8,128)(2,1)}, u32[]{:S(2)}) copy-start(bf16[256,256]{1,0:T(8,128)(2,1)} %param.13) | copy-start | bytes 393220
  321.0 84.9 %all-to-all-start.8 = ((f32[2,32,8,256]{3,2,0,1:T(8,128)}), f32[2,32,8,256]{3,2,0,1:T(8,128)S(1)}, u32[]{:S(2)}, u32[]{:S(2)}) async-start(f32[2,32,8,256]{3,2,0,1:T(8,128)} %copy.64), calls=%async_computation.8 | async-start | bytes 1048576 | tf_op jit(solution)/shard_map/all_to_all | solution.py:105
  406.8 5.5 collective-permute-start.1
